TPU v7x, 32 devices: a whole 2x2x4 slice. The times are simulated.
32 devices in a mesh: dp: 8 (over z, x), ctx: 4 (over y, core).
Axes of the slice: x: 2, y: 2, z: 4, core: 2. Of those that a mesh axis runs over, the one named last changes fastest.
Arguments:
- queries: bfloat16 [8, 2048, 1280], P('dp', 'ctx'), may hold values from -14 to 14
- own_keys: bfloat16 [8, 2048, 1280], P('dp', 'ctx'), may hold values from -6 to 6
- own_values: bfloat16 [8, 2048, 1280], P('dp', 'ctx'), may hold values from -12 to 12
- variant_blocks: int32 [8, 4, 6], P('dp', 'ctx'), may hold values from 1 to 2, 8 in all within a row
- db_keys: bfloat16 [8, 256, 1280], P('dp', 'ctx'), may hold values from -6 to 6
- db_values: bfloat16 [8, 256, 1280], P('dp', 'ctx'), may hold values from -12 to 12
- ret_shard: int32 [8, 64], P(None, 'ctx'), may hold values from 0 to 7, as said below
- ret_block: int32 [8, 64], P(None, 'ctx'), may hold values from 0 to 15
Outputs:
- attended: bfloat16 [8, 2048, 1280], P('dp', 'ctx')
Inputs may be any that keep to these rules, and one draw needn't show every extreme that they name: `ret_shard`: within each aligned block of 16 entries of a row (the retrieval blocks of one context device), no shard is named more than 4 times, and some shard is named exactly 4 times.
All inputs are finite; a program needn't handle non-finite values.
Results may differ from a plain program's by a relative error of at most 0.0035.
Values may be sent and summed in bfloat16 or wider, within the bound.
No kernel may reach another device: no remote copies, remote signals or barrier semaphores. Data moves between devices by JAX's collectives and lax.ppermute only.
A program may use at most 192 MiB of HBM per device.

v0:
```python
import functools
import math

import jax
import jax.numpy as jnp
from jax import lax
from jax.experimental import pallas as pl
from jax.experimental.pallas import tpu as pltpu
from jax.sharding import PartitionSpec as P


HEAD_DIM = 128
BLK = 64
ROW_BLK = 4


PARAMS = pltpu.CompilerParams(vmem_limit_bytes=16 << 20)
SMEM = pl.BlockSpec(memory_space=pltpu.SMEM)
VMEM = pl.BlockSpec(memory_space=pltpu.VMEM)
HBM = pl.BlockSpec(memory_space=pltpu.HBM)
SCALE = math.log2(math.e) / math.sqrt(HEAD_DIM)
NT = (((1,), (1,)), ((), ()))
masked_score = -1e30


def iota(shape, dim):
    return lax.broadcasted_iota(jnp.int32, shape, dim)


def pick(matrix, rows):
    return jnp.dot(matrix.astype(jnp.bfloat16), rows, preferred_element_type=jnp.float32).astype(
        jnp.bfloat16
    )


def pack_kernel(capacity, me_ref, shard_hbm, block_hbm, keys_hbm, values_hbm, *refs):
    out_refs, (shard_ref, block_ref, rows_ref, sems) = refs[:-4], refs[-4:]
    me = me_ref[0]
    slots = shard_ref.shape[1]
    tokens = keys_hbm.shape[0]
    half = capacity * ROW_BLK
    copies = [
        pltpu.make_async_copy(source, target, sems.at[number])
        for number, (source, target) in enumerate(
            (
                (shard_hbm, shard_ref),
                (block_hbm, block_ref),
                (keys_hbm, rows_ref.at[0:tokens]),
                (values_hbm, rows_ref.at[tokens : 2 * tokens]),
            )
        )
    ]
    for copy in copies:
        copy.start()
    for copy in copies:
        copy.wait()
    rows = rows_ref[...]
    row = iota((2 * half, slots), 0)
    level = (row % half) // ROW_BLK
    before = (iota((slots, slots), 0) < iota((slots, slots), 1)).astype(jnp.float32)
    mine_all = (shard_ref[...] == me).astype(jnp.float32)
    earlier_all = jnp.dot(mine_all, before, preferred_element_type=jnp.float32)
    wanted_all = jnp.where(mine_all > 0, earlier_all.astype(jnp.int32), -1)
    line = iota((2 * half, 1), 0)
    base = (line // half) * tokens + line % ROW_BLK
    column = iota((2 * half, 2 * tokens), 1)
    member = iota(wanted_all.shape, 0)
    for distance, out_ref in enumerate(out_refs):
        group = me ^ distance
        here = member == group
        wanted = jnp.sum(jnp.where(here, wanted_all, 0), axis=0, keepdims=True)
        blocks = jnp.sum(jnp.where(here, block_ref[...], 0), axis=0, keepdims=True)
        source = jnp.sum(jnp.where(wanted == level, blocks, 0), axis=1, keepdims=True)
        out_ref[...] = pick(column == base + source * ROW_BLK, rows)


def compact_kernel(capacity, me_ref, shard_ref, after_ref, *refs):
    piece_refs, (keys_ref, values_ref) = refs[:-2], refs[-2:]
    me = me_ref[0]
    slots = shard_ref.shape[1]
    half = capacity * ROW_BLK
    tokens = slots * ROW_BLK
    pieces = jnp.concatenate([piece_ref[...] for piece_ref in piece_refs], axis=0)
    here = iota(shard_ref.shape, 0) == me
    shards = jnp.sum(jnp.where(here, shard_ref[...], 0), axis=0, keepdims=True)
    slot = iota((tokens, slots), 0) // ROW_BLK
    lane = iota((tokens, slots), 1)
    named = jnp.sum(jnp.where(lane == slot, shards, 0), axis=1, keepdims=True)
    level = jnp.sum(((shards == named) & (lane < slot)).astype(jnp.int32), axis=1, keepdims=True)
    inside = iota((tokens, 1), 0) % ROW_BLK
    target = (named ^ me) * (2 * half) + level * ROW_BLK + inside
    column = iota((tokens, pieces.shape[0]), 1)
    keys_ref[...] = pick(column == target, pieces)
    values_ref[...] = pick(column == target + half, pieces)


def weigh(weights, values):
    both = jnp.concatenate([values, jnp.ones_like(values)], axis=1)
    result = jnp.dot(weights, both, preferred_element_type=jnp.float32)
    return result[:, :HEAD_DIM], result[:, HEAD_DIM:]


def own_kernel(
    lengths_ref,
    q_hbm,
    keys_hbm,
    values_hbm,
    after_ref,
    query_ref,
    acc_ref,
    largest_ref,
    total_ref,
    mask_ref,
    keys_ref,
    values_ref,
    weights_ref,
    sems,
):
    copies = [
        pltpu.make_async_copy(source, target, sems.at[number])
        for number, (source, target) in enumerate(
            ((q_hbm, query_ref), (keys_hbm, keys_ref), (values_hbm, values_ref))
        )
    ]
    for copy in copies:
        copy.start()
    count, features = query_ref.shape
    blocks = count // BLK
    starts = [max(0, block - 1) * BLK for block in range(blocks)]
    row = iota((BLK, 2 * BLK), 0)
    column = iota((BLK, 2 * BLK), 1)
    mask_ref[0:BLK, :] = jnp.where(column <= row, 0.0, masked_score)
    for block in range(1, blocks):
        end = jnp.int32(0)
        opens = jnp.int32(0)
        for variant in range(lengths_ref.shape[0]):
            end = end + lengths_ref[variant]
            opens = opens + (end == block).astype(jnp.int32)
        first = jnp.where(opens > 0, BLK, 0)
        allowed = (column <= row + BLK) & (column >= first)
        mask_ref[block * BLK : (block + 1) * BLK, :] = jnp.where(allowed, 0.0, masked_score)
    for copy in copies:
        copy.wait()
    for head in range(features // HEAD_DIM):
        lanes = slice(head * HEAD_DIM, (head + 1) * HEAD_DIM)
        for block in range(blocks):
            rows = slice(block * BLK, (block + 1) * BLK)
            acc_ref[rows, lanes] = lax.dot_general(
                query_ref[rows, lanes],
                keys_ref[starts[block] : starts[block] + 2 * BLK, lanes],
                NT,
                preferred_element_type=jnp.float32,
            )
    for head in range(features // HEAD_DIM):
        lanes = slice(head * HEAD_DIM, (head + 1) * HEAD_DIM)
        scores = acc_ref[:, lanes] * SCALE + mask_ref[...]
        largest = jnp.max(scores, axis=1, keepdims=True)
        weights = jnp.exp2(scores - largest)
        weights_ref[:, lanes] = weights.astype(jnp.bfloat16)
        largest_ref[:, lanes] = jnp.broadcast_to(largest, (count, HEAD_DIM))
    for head in range(features // HEAD_DIM):
        lanes = slice(head * HEAD_DIM, (head + 1) * HEAD_DIM)
        for block in range(blocks):
            rows = slice(block * BLK, (block + 1) * BLK)
            acc_ref[rows, lanes], total_ref[rows, lanes] = weigh(
                weights_ref[rows, lanes], values_ref[starts[block] : starts[block] + 2 * BLK, lanes]
            )


LAZY = 60.0


def context_kernel(last, query_ref, acc_ref, largest_ref, total_ref, *refs):
    out_count = 4 if last else 3
    refs, out_refs = refs[:-out_count], refs[-out_count:]
    if last:
        key_refs, value_refs = refs, None
        weights_ref, new_acc_ref, new_largest_ref, inverse_ref = out_refs
    else:
        key_refs, value_refs = refs[: len(refs) // 2], refs[len(refs) // 2 :]
        new_acc_ref, new_largest_ref, new_total_ref = out_refs
    features = query_ref.shape[1]

    def absorb(exact):
        excess = None
        for head in range(features // HEAD_DIM):
            lanes = slice(head * HEAD_DIM, (head + 1) * HEAD_DIM)
            keys = jnp.concatenate([key_ref[:, lanes] for key_ref in key_refs], axis=0)
            scores = lax.dot_general(
                query_ref[:, lanes], keys, NT, preferred_element_type=jnp.float32
            )
            scores = scores * SCALE
            largest = new_largest_ref[:, lanes]
            acc, total = (new_acc_ref if last else acc_ref)[:, lanes], total_ref[:, lanes]
            if exact:
                before = largest
                largest = jnp.maximum(before, jnp.max(scores, axis=1, keepdims=True))
                rescale = jnp.exp2(before - largest)
                acc, total = acc * rescale, total * rescale
                new_largest_ref[:, lanes] = largest
            scores = scores - largest[:, :1]
            if not exact:
                highest = functools.reduce(
                    jnp.maximum,
                    [scores[start : start + BLK] for start in range(0, scores.shape[0], BLK)],
                )
                excess = highest if excess is None else jnp.maximum(excess, highest)
            weights = jnp.exp2(scores).astype(jnp.bfloat16)
            if last:
                weights_ref[head] = weights
                ones = jnp.ones((keys.shape[0], HEAD_DIM), weights.dtype)
                more = jnp.dot(weights, ones, preferred_element_type=jnp.float32)
                inverse_ref[:, lanes] = 1.0 / (total + more)
                if exact:
                    new_acc_ref[:, lanes] = acc
            else:
                values = jnp.concatenate([value_ref[:, lanes] for value_ref in value_refs], axis=0)
                more_acc, more = weigh(weights, values)
                new_acc_ref[:, lanes] = acc + more_acc
                new_total_ref[:, lanes] = total + more
        return excess

    excess = jnp.max(absorb(False))

    @pl.when(excess > LAZY)
    def _():
        absorb(True)


def value_kernel(scaled_ref, weights_ref, inverse_ref, *refs):
    value_refs, (out_hbm, out_ref, sems) = refs[:-3], refs[-3:]
    _, features = scaled_ref.shape
    copies = []
    for head in range(features // HEAD_DIM):
        lanes = slice(head * HEAD_DIM, (head + 1) * HEAD_DIM)
        values = jnp.concatenate([value_ref[:, lanes] for value_ref in value_refs], axis=0)
        attended = scaled_ref[:, lanes] + jnp.dot(
            weights_ref[head], values, preferred_element_type=jnp.float32
        )
        out_ref[:, lanes] = (attended * inverse_ref[:, lanes]).astype(out_ref.dtype)
        copies.append(
            pltpu.make_async_copy(out_ref.at[:, lanes], out_hbm.at[:, lanes], sems.at[head])
        )
        copies[-1].start()
    for copy in copies:
        copy.wait()


def hbm(array):
    return pltpu.with_memory_space_constraint(array, pltpu.HBM)


def swap(array, axis, distance):
    size = lax.axis_size(axis)
    return lax.ppermute(array, axis, [(i, i ^ distance) for i in range(size)])


def gather_pair(keys, values):
    return (keys, values), (swap(keys, "ctx", 1), swap(values, "ctx", 1))


def per_device(
    queries, own_keys, own_values, variant_blocks, db_keys, db_values, ret_shard, ret_block
):
    count, features = queries.shape[1:]
    heads = features // HEAD_DIM
    groups = lax.axis_size("dp")
    columns = lax.axis_size("ctx")
    slots = ret_shard.shape[1]
    tokens = slots * ROW_BLK
    capacity = max(2, 2 * slots // groups)
    me = lax.axis_index("dp").astype(jnp.int32).reshape(1)
    bf16 = jnp.bfloat16
    wide = jax.ShapeDtypeStruct((count, features), jnp.float32)
    piece = jax.ShapeDtypeStruct((2 * capacity * ROW_BLK, features), bf16)

    sent = pl.pallas_call(
        lambda *refs: pack_kernel(capacity, *refs),
        out_shape=[piece] * groups,
        in_specs=[SMEM] + [HBM] * 4,
        out_specs=[VMEM] * groups,
        scratch_shapes=[
            pltpu.VMEM(ret_shard.shape, jnp.int32),
            pltpu.VMEM(ret_block.shape, jnp.int32),
            pltpu.VMEM((2 * tokens, features), bf16),
            pltpu.SemaphoreType.DMA((4,)),
        ],
        name="pack",
        compiler_params=PARAMS,
    )(me, hbm(ret_shard), hbm(ret_block), hbm(db_keys[0]), hbm(db_values[0]))
    pieces = [sent[0]]
    for distance in range(1, groups):
        pieces.append(swap(sent[distance], "dp", distance))
    query, acc, largest, total = pl.pallas_call(
        own_kernel,
        out_shape=[jax.ShapeDtypeStruct((count, features), bf16)] + [wide] * 3,
        in_specs=[SMEM] + [HBM] * 3 + [VMEM],
        out_specs=[VMEM] * 4,
        scratch_shapes=[
            pltpu.VMEM((count, 2 * BLK), jnp.float32),
            pltpu.VMEM((count, features), bf16),
            pltpu.VMEM((count, features), bf16),
            pltpu.VMEM((count, features), bf16),
            pltpu.SemaphoreType.DMA((3,)),
        ],
        name="own",
        compiler_params=PARAMS,
        cost_estimate=pl.CostEstimate(
            flops=4 * count * 2 * BLK * features,
            transcendentals=2 * count * BLK * heads,
            bytes_accessed=20 * count * features,
        ),
    )(variant_blocks[0, 0], hbm(queries[0]), hbm(own_keys[0]), hbm(own_values[0]), sent[0])
    row_block = jax.ShapeDtypeStruct((tokens, features), bf16)
    keys, values = pl.pallas_call(
        lambda *refs: compact_kernel(capacity, *refs),
        out_shape=[row_block] * 2,
        in_specs=[SMEM] + [VMEM] * (2 + groups),
        out_specs=[VMEM] * 2,
        name="compact",
        compiler_params=PARAMS,
    )(me, ret_shard, total, *pieces)
    far = []
    distance = columns // 2
    while distance > 1:
        far_keys = [swap(one, "ctx", distance) for one in [keys] + [k for k, _ in far]]
        far_values = [swap(one, "ctx", distance) for one in [values] + [v for _, v in far]]
        far = far + list(zip(far_keys, far_values))
        distance //= 2
    near = gather_pair(keys, values)
    far = [pair for one in far for pair in gather_pair(*one)]
    acc, largest, total = pl.pallas_call(
        lambda *refs: context_kernel(False, *refs),
        out_shape=[wide] * 3,
        in_specs=[VMEM] * (4 + 2 * len(near)),
        out_specs=[VMEM] * 3,
        input_output_aliases={2: 1},
        name="near",
        compiler_params=PARAMS,
    )(query, acc, largest, total, *[k for k, _ in near], *[v for _, v in near])
    weights, acc, largest, inverse = pl.pallas_call(
        lambda *refs: context_kernel(True, *refs),
        out_shape=[jax.ShapeDtypeStruct((heads, count, len(far) * tokens), bf16)] + [wide] * 3,
        in_specs=[VMEM] * (4 + len(far)),
        out_specs=[VMEM] * 4,
        input_output_aliases={1: 1, 2: 2},
        name="score",
        compiler_params=PARAMS,
    )(query, acc, largest, total, *[k for k, _ in far])
    attended = pl.pallas_call(
        value_kernel,
        out_shape=jax.ShapeDtypeStruct((count, features), bf16),
        in_specs=[VMEM] * (3 + len(far)),
        out_specs=HBM,
        scratch_shapes=[
            pltpu.VMEM((count, features), bf16),
            pltpu.SemaphoreType.DMA((heads,)),
        ],
        name="value",
        compiler_params=PARAMS,
    )(acc, weights, inverse, *[v for _, v in far])
    return attended[None]


def solution(mesh):
    split = P("dp", "ctx", None)
    return jax.shard_map(
        per_device,
        mesh=mesh,
        in_specs=(split,) * 6 + (P(None, "ctx"),) * 2,
        out_specs=split,
        check_vma=False,
    )
```

profile of v0, /device:TPU:17, one launch (start us, length us, event | category | flops | bytes accessed | tf_op | source)
XLA Modules:
  0.0 42.0 jit_solution(16057849306918562683)
XLA Ops:
  0.0 1.7 %pack.1 = (bf16[32,1280]{1,0:T(8,128)(2,1)S(1)}, bf16[32,1280]{1,0:T(8,128)(2,1)S(1)}, bf16[32,1280]{1,0:T(8,128)(2,1)S(1)}, bf16[32,1280]{1,0:T(8,128)(2,1)S(1)...) custom-call(s32[1]{0:T(128)} %bitcast.4.refs_0_, ...), custom_call_target="tpu_custom_call" | custom-call | tf_op jit(solution)/shard_map/pack/pallas_call | solution.py:277
  1.8 1.3 %collective-permute-start = (bf16[32,1280]{1,0:T(8,128)(2,1)S(1)}, bf16[32,1280]{1,0:T(8,128)(2,1)S(1)}, u32[]{:S(2)}, u32[]{:S(2)}) collective-permute-start(bf16[32,1280]{1,0:T(8,128)(2,1)S(1)} %get-tuple-element.30), channel_id=1, source_target_pairs={{0,4},{4,0},{8,12},{12,8},{16,20},{20,16},{24,28},{28,24},{1,5},{5... | collective-permute-start | bytes 245768 | tf_op jit(solution)/shard_map/ppermute | solution.py:255
  3.0 1.3 %collective-permute-start.1 = (bf16[32,1280]{1,0:T(8,128)(2,1)S(1)}, bf16[32,1280]{1,0:T(8,128)(2,1)S(1)}, u32[]{:S(2)}, u32[]{:S(2)}) collective-permute-start(bf16[32,1280]{1,0:T(8,128)(2,1)S(1)} %get-tuple-element.31), channel_id=1, source_target_pairs={{0,8},{4,12},{8,0},{12,4},{16,24},{20,28},{24,16},{28,20},{1,9},{5... | collective-permute-start | bytes 245768 | tf_op jit(solution)/shard_map/ppermute | solution.py:255
  4.3 0.1 collective-permute-start.2
  4.5 3.3 %collective-permute-start.4 = (bf16[32,1280]{1,0:T(8,128)(2,1)S(1)}, bf16[32,1280]{1,0:T(8,128)(2,1)S(1)}, u32[]{:S(2)}, u32[]{:S(2)}) collective-permute-start(bf16[32,1280]{1,0:T(8,128)(2,1)S(1)} %get-tuple-element.34), channel_id=1, source_target_pairs={{0,20},{4,16},{8,28},{12,24},{16,4},{20,0},{24,12},{28,8},{1,21},{... | collective-permute-start | bytes 245768 | tf_op jit(solution)/shard_map/ppermute | solution.py:255
  7.8 0.0 collective-permute-done.refs_4_
  7.8 0.2 collective-permute-start.5
  7.9 0.0 collective-permute-done.1.refs_5_
  7.9 1.3 %collective-permute-start.6 = (bf16[32,1280]{1,0:T(8,128)(2,1)S(1)}, bf16[32,1280]{1,0:T(8,128)(2,1)S(1)}, u32[]{:S(2)}, u32[]{:S(2)}) collective-permute-start(bf16[32,1280]{1,0:T(8,128)(2,1)S(1)} %get-tuple-element.36), channel_id=1, source_target_pairs={{0,28},{4,24},{8,20},{12,16},{16,12},{20,8},{24,4},{28,0},{1,29},{... | collective-permute-start | bytes 245768 | tf_op jit(solution)/shard_map/ppermute | solution.py:255
  9.2 0.7 %copy-done.1 = s32[1,1,6]{2,1,0:T(1,128)S(1)} copy-done((s32[1,1,6]{2,1,0:T(1,128)S(1)}, s32[1,1,6]{2,1,0:T(1,128)}, u32[]{:S(2)}) %copy-start.1) | copy-done | bytes 48
  9.9 5.3 %own.1 = (bf16[512,1280]{1,0:T(8,128)(2,1)S(1)}, f32[512,1280]{1,0:T(8,128)S(1)}, f32[512,1280]{1,0:T(8,128)S(1)}, f32[512,1280]{1,0:T(8,128)S(1)}) custom-call(s32[6]{0:T(128)S(1)} %bitcast.8, bf16[512,1280]{1,0:T(8,128)(2,1)} %bitcast.9, bf16[512,1280]{1,0:T(8,128)(2,1)} %bitcast.10, bf16[512,1280]{1,0:T(8,128)(2,1)} %bitcast.11, ...), custom_call_target="tpu_custom_call" | custom-call | flops 335544320 | bytes 13107200 | tf_op jit(solution)/shard_map/own/pallas_call | solution.py:294
  15.2 3.9 %collective-permute-done.5.refs_9_ = bf16[32,1280]{1,0:T(8,128)(2,1)S(1)} collective-permute-done((bf16[32,1280]{1,0:T(8,128)(2,1)S(1)}, bf16[32,1280]{1,0:T(8,128)(2,1)S(1)}, u32[]{:S(2)}, u32[]{:S(2)}) %collective-permute-start.5) | collective-permute-done | bytes 81952 | tf_op jit(solution)/shard_map/ppermute | solution.py:255
  19.1 3.6 %collective-permute-done.6.refs_10_ = bf16[32,1280]{1,0:T(8,128)(2,1)S(1)} collective-permute-done((bf16[32,1280]{1,0:T(8,128)(2,1)S(1)}, bf16[32,1280]{1,0:T(8,128)(2,1)S(1)}, u32[]{:S(2)}, u32[]{:S(2)}) %collective-permute-start.6) | collective-permute-done | bytes 81952 | tf_op jit(solution)/shard_map/ppermute | solution.py:255
  22.7 0.5 %compact.1 = (bf16[64,1280]{1,0:T(8,128)(2,1)S(1)}, bf16[64,1280]{1,0:T(8,128)(2,1)S(1)}) custom-call(s32[1]{0:T(128)} %bitcast.4.refs_0_, s32[8,16]{1,0:T(8,128)S(1)} %copy-done, f32[512,1280]{1,0:T(8,128)S(1)} %get-tuple-element.29.refs_2_.refs_3_, bf16[32,1280]{1,0:T(8,128)(2,1)S(1)} %get-tuple-element.25.after_ref.refs_3_, ...), custom_call_target="tpu_custom_call" | custom-call | tf_op jit(solution)/shard_map/compact/pallas_call | solution.py:315
  23.2 1.3 %collective-permute-start.9 = (bf16[64,1280]{1,0:T(8,128)(2,1)S(1)}, bf16[64,1280]{1,0:T(8,128)(2,1)S(1)}, u32[]{:S(2)}, u32[]{:S(2)}) collective-permute-start(bf16[64,1280]{1,0:T(8,128)(2,1)S(1)} %get-tuple-element.37.refs_4_), channel_id=1, source_target_pairs={{0,2},{1,3},{2,0},{3,1},{4,6},{5,7},{6,4},{7,5},{8,10},{9,11},{10,... | collective-permute-start | bytes 491528 | tf_op jit(solution)/shard_map/ppermute | solution.py:255
  24.5 0.2 collective-permute-start.11
  24.8 1.3 %collective-permute-start.7 = (bf16[64,1280]{1,0:T(8,128)(2,1)S(1)}, bf16[64,1280]{1,0:T(8,128)(2,1)S(1)}, u32[]{:S(2)}, u32[]{:S(2)}) collective-permute-start(bf16[64,1280]{1,0:T(8,128)(2,1)S(1)} %get-tuple-element.37.refs_4_), channel_id=1, source_target_pairs={{0,1},{1,0},{2,3},{3,2},{4,5},{5,4},{6,7},{7,6},{8,9},{9,8},{10,11... | collective-permute-start | bytes 491528 | tf_op jit(solution)/shard_map/ppermute | solution.py:255
  26.1 2.2 %collective-permute-done.9.refs_4_ = bf16[64,1280]{1,0:T(8,128)(2,1)S(1)} collective-permute-done((bf16[64,1280]{1,0:T(8,128)(2,1)S(1)}, bf16[64,1280]{1,0:T(8,128)(2,1)S(1)}, u32[]{:S(2)}, u32[]{:S(2)}) %collective-permute-start.9) | collective-permute-done | bytes 163872 | tf_op jit(solution)/shard_map/ppermute | solution.py:255
  28.3 2.8 %collective-permute-start.10 = (bf16[64,1280]{1,0:T(8,128)(2,1)S(1)}, bf16[64,1280]{1,0:T(8,128)(2,1)S(1)}, u32[]{:S(2)}, u32[]{:S(2)}) collective-permute-start(bf16[64,1280]{1,0:T(8,128)(2,1)S(1)} %collective-permute-done.9.refs_4_), channel_id=1, source_target_pairs={{0,1},{1,0},{2,3},{3,2},{4,5},{5,4},{6,7},{7,6},{8,9},{9,8},{10,11... | collective-permute-start | bytes 491528 | tf_op jit(solution)/shard_map/ppermute | solution.py:255
  31.1 0.7 %collective-permute-done.11.refs_0_ = bf16[64,1280]{1,0:T(8,128)(2,1)S(1)} collective-permute-done((bf16[64,1280]{1,0:T(8,128)(2,1)S(1)}, bf16[64,1280]{1,0:T(8,128)(2,1)S(1)}, u32[]{:S(2)}, u32[]{:S(2)}) %collective-permute-start.11) | collective-permute-done | bytes 163872 | tf_op jit(solution)/shard_map/ppermute | solution.py:255
  31.8 1.6 %collective-permute-start.12 = (bf16[64,1280]{1,0:T(8,128)(2,1)S(1)}, bf16[64,1280]{1,0:T(8,128)(2,1)S(1)}, u32[]{:S(2)}, u32[]{:S(2)}) collective-permute-start(bf16[64,1280]{1,0:T(8,128)(2,1)S(1)} %collective-permute-done.11.refs_0_), channel_id=1, source_target_pairs={{0,1},{1,0},{2,3},{3,2},{4,5},{5,4},{6,7},{7,6},{8,9},{9,8},{10,11... | collective-permute-start | bytes 491528 | tf_op jit(solution)/shard_map/ppermute | solution.py:255
  33.4 5.6 %near.1 = (f32[512,1280]{1,0:T(8,128)S(1)}, f32[512,1280]{1,0:T(8,128)S(1)}, f32[512,1280]{1,0:T(8,128)S(1)}) custom-call(bf16[512,1280]{1,0:T(8,128)(2,1)S(1)} %get-tuple-element.26.refs_0_, f32[512,1280]{1,0:T(8,128)S(1)} %get-tuple-element.27.refs_1_, f32[512,1280]{1,0:T(8,128)S(1)} %get-tuple-element.28.refs_2_, ...), custom_call_target="tpu_custom_call", output_to_operand_aliasing={{1}: (2, {})} | custom-call | tf_op jit(solution)/shard_map/near/pallas_call | solution.py:332
  39.1 1.4 %score.1 = (bf16[10,512,128]{2,1,0:T(8,128)(2,1)S(1)}, f32[512,1280]{1,0:T(8,128)S(1)}, f32[512,1280]{1,0:T(8,128)S(1)}, f32[512,1280]{1,0:T(8,128)S(1)}) custom-call(bf16[512,1280]{1,0:T(8,128)(2,1)S(1)} %get-tuple-element.26.refs_0_, f32[512,1280]{1,0:T(8,128)S(1)} %get-tuple-element.39.refs_1_, ...), custom_call_target="tpu_custom_call", output_to_operand_aliasing={{1}: (1, {}), {2}: (2, {})} | custom-call | tf_op jit(solution)/shard_map/score/pallas_call | solution.py:341
  40.5 1.4 %value.1 = bf16[512,1280]{1,0:T(8,128)(2,1)} custom-call(f32[512,1280]{1,0:T(8,128)S(1)} %get-tuple-element.42.scaled_ref, bf16[10,512,128]{2,1,0:T(8,128)(2,1)S(1)} %get-tuple-element.43.weights_ref, f32[512,1280]{1,0:T(8,128)S(1)} %get-tuple-element.44.inverse_ref, bf16[64,1280]{1,0:T(8,128)(2,1)S(1)} %collective-permute-done.11.refs_0_, ...), custom_call_target="tpu_custom_call" | custom-call | tf_op jit(solution)/shard_map/value/pallas_call | solution.py:350
  (12 shorter events, 0.0 us)
Async XLA Ops:
  0.0 22.7 %copy-start = (s32[8,16]{1,0:T(8,128)S(1)}, s32[8,16]{1,0:T(8,128)}, u32[]{:S(2)}) copy-start(s32[8,16]{1,0:T(8,128)} %refs_1_.3) | copy-start | bytes 1540
  1.8 6.0 %collective-permute-start = (bf16[32,1280]{1,0:T(8,128)(2,1)S(1)}, bf16[32,1280]{1,0:T(8,128)(2,1)S(1)}, u32[]{:S(2)}, u32[]{:S(2)}) collective-permute-start(bf16[32,1280]{1,0:T(8,128)(2,1)S(1)} %get-tuple-element.30), channel_id=1, source_target_pairs={{0,4},{4,0},{8,12},{12,8},{16,20},{20,16},{24,28},{28,24},{1,5},{5... | collective-permute-start | bytes 245768 | tf_op jit(solution)/shard_map/ppermute | solution.py:255
  3.0 4.9 %collective-permute-start.1 = (bf16[32,1280]{1,0:T(8,128)(2,1)S(1)}, bf16[32,1280]{1,0:T(8,128)(2,1)S(1)}, u32[]{:S(2)}, u32[]{:S(2)}) collective-permute-start(bf16[32,1280]{1,0:T(8,128)(2,1)S(1)} %get-tuple-element.31), channel_id=1, source_target_pairs={{0,8},{4,12},{8,0},{12,4},{16,24},{20,28},{24,16},{28,20},{1,9},{5... | collective-permute-start | bytes 245768 | tf_op jit(solution)/shard_map/ppermute | solution.py:255
  4.3 10.9 %collective-permute-start.2 = (bf16[32,1280]{1,0:T(8,128)(2,1)S(1)}, bf16[32,1280]{1,0:T(8,128)(2,1)S(1)}, u32[]{:S(2)}, u32[]{:S(2)}) collective-permute-start(bf16[32,1280]{1,0:T(8,128)(2,1)S(1)} %get-tuple-element.32), channel_id=1, source_target_pairs={{0,12},{4,8},{8,4},{12,0},{16,28},{20,24},{24,20},{28,16},{1,13},{... | collective-permute-start | bytes 245768 | tf_op jit(solution)/shard_map/ppermute | solution.py:255
  4.5 10.7 %collective-permute-start.3 = (bf16[32,1280]{1,0:T(8,128)(2,1)S(1)}, bf16[32,1280]{1,0:T(8,128)(2,1)S(1)}, u32[]{:S(2)}, u32[]{:S(2)}) collective-permute-start(bf16[32,1280]{1,0:T(8,128)(2,1)S(1)} %get-tuple-element.33), channel_id=1, source_target_pairs={{0,16},{4,20},{8,24},{12,28},{16,0},{20,4},{24,8},{28,12},{1,17},{... | collective-permute-start | bytes 245768 | tf_op jit(solution)/shard_map/ppermute | solution.py:255
  4.5 10.8 %collective-permute-start.4 = (bf16[32,1280]{1,0:T(8,128)(2,1)S(1)}, bf16[32,1280]{1,0:T(8,128)(2,1)S(1)}, u32[]{:S(2)}, u32[]{:S(2)}) collective-permute-start(bf16[32,1280]{1,0:T(8,128)(2,1)S(1)} %get-tuple-element.34), channel_id=1, source_target_pairs={{0,20},{4,16},{8,28},{12,24},{16,4},{20,0},{24,12},{28,8},{1,21},{... | collective-permute-start | bytes 245768 | tf_op jit(solution)/shard_map/ppermute | solution.py:255
  7.8 11.4 %collective-permute-start.5 = (bf16[32,1280]{1,0:T(8,128)(2,1)S(1)}, bf16[32,1280]{1,0:T(8,128)(2,1)S(1)}, u32[]{:S(2)}, u32[]{:S(2)}) collective-permute-start(bf16[32,1280]{1,0:T(8,128)(2,1)S(1)} %get-tuple-element.35), channel_id=1, source_target_pairs={{0,24},{4,28},{8,16},{12,20},{16,8},{20,12},{24,0},{28,4},{1,25},{... | collective-permute-start | bytes 245768 | tf_op jit(solution)/shard_map/ppermute | solution.py:255
  7.9 14.8 %collective-permute-start.6 = (bf16[32,1280]{1,0:T(8,128)(2,1)S(1)}, bf16[32,1280]{1,0:T(8,128)(2,1)S(1)}, u32[]{:S(2)}, u32[]{:S(2)}) collective-permute-start(bf16[32,1280]{1,0:T(8,128)(2,1)S(1)} %get-tuple-element.36), channel_id=1, source_target_pairs={{0,28},{4,24},{8,20},{12,16},{16,12},{20,8},{24,4},{28,0},{1,29},{... | collective-permute-start | bytes 245768 | tf_op jit(solution)/shard_map/ppermute | solution.py:255
  9.2 0.7 %copy-start.1 = (s32[1,1,6]{2,1,0:T(1,128)S(1)}, s32[1,1,6]{2,1,0:T(1,128)}, u32[]{:S(2)}) copy-start(s32[1,1,6]{2,1,0:T(1,128)} %param.11) | copy-start | bytes 76
  23.2 5.1 %collective-permute-start.9 = (bf16[64,1280]{1,0:T(8,128)(2,1)S(1)}, bf16[64,1280]{1,0:T(8,128)(2,1)S(1)}, u32[]{:S(2)}, u32[]{:S(2)}) collective-permute-start(bf16[64,1280]{1,0:T(8,128)(2,1)S(1)} %get-tuple-element.37.refs_4_), channel_id=1, source_target_pairs={{0,2},{1,3},{2,0},{3,1},{4,6},{5,7},{6,4},{7,5},{8,10},{9,11},{10,... | collective-permute-start | bytes 491528 | tf_op jit(solution)/shard_map/ppermute | solution.py:255
  24.5 7.3 %collective-permute-start.11 = (bf16[64,1280]{1,0:T(8,128)(2,1)S(1)}, bf16[64,1280]{1,0:T(8,128)(2,1)S(1)}, u32[]{:S(2)}, u32[]{:S(2)}) collective-permute-start(bf16[64,1280]{1,0:T(8,128)(2,1)S(1)} %get-tuple-element.38.refs_6_), channel_id=1, source_target_pairs={{0,2},{1,3},{2,0},{3,1},{4,6},{5,7},{6,4},{7,5},{8,10},{9,11},{10,... | collective-permute-start | bytes 491528 | tf_op jit(solution)/shard_map/ppermute | solution.py:255
  24.8 8.7 %collective-permute-start.7 = (bf16[64,1280]{1,0:T(8,128)(2,1)S(1)}, bf16[64,1280]{1,0:T(8,128)(2,1)S(1)}, u32[]{:S(2)}, u32[]{:S(2)}) collective-permute-start(bf16[64,1280]{1,0:T(8,128)(2,1)S(1)} %get-tuple-element.37.refs_4_), channel_id=1, source_target_pairs={{0,1},{1,0},{2,3},{3,2},{4,5},{5,4},{6,7},{7,6},{8,9},{9,8},{10,11... | collective-permute-start | bytes 491528 | tf_op jit(solution)/shard_map/ppermute | solution.py:255
  26.1 7.3 %collective-permute-start.8 = (bf16[64,1280]{1,0:T(8,128)(2,1)S(1)}, bf16[64,1280]{1,0:T(8,128)(2,1)S(1)}, u32[]{:S(2)}, u32[]{:S(2)}) collective-permute-start(bf16[64,1280]{1,0:T(8,128)(2,1)S(1)} %get-tuple-element.38.refs_6_), channel_id=1, source_target_pairs={{0,1},{1,0},{2,3},{3,2},{4,5},{5,4},{6,7},{7,6},{8,9},{9,8},{10,11... | collective-permute-start | bytes 491528 | tf_op jit(solution)/shard_map/ppermute | solution.py:255
  28.3 10.8 %collective-permute-start.10 = (bf16[64,1280]{1,0:T(8,128)(2,1)S(1)}, bf16[64,1280]{1,0:T(8,128)(2,1)S(1)}, u32[]{:S(2)}, u32[]{:S(2)}) collective-permute-start(bf16[64,1280]{1,0:T(8,128)(2,1)S(1)} %collective-permute-done.9.refs_4_), channel_id=1, source_target_pairs={{0,1},{1,0},{2,3},{3,2},{4,5},{5,4},{6,7},{7,6},{8,9},{9,8},{10,11... | collective-permute-start | bytes 491528 | tf_op jit(solution)/shard_map/ppermute | solution.py:255
  31.8 8.7 %collective-permute-start.12 = (bf16[64,1280]{1,0:T(8,128)(2,1)S(1)}, bf16[64,1280]{1,0:T(8,128)(2,1)S(1)}, u32[]{:S(2)}, u32[]{:S(2)}) collective-permute-start(bf16[64,1280]{1,0:T(8,128)(2,1)S(1)} %collective-permute-done.11.refs_0_), channel_id=1, source_target_pairs={{0,1},{1,0},{2,3},{3,2},{4,5},{5,4},{6,7},{7,6},{8,9},{9,8},{10,11... | collective-permute-start | bytes 491528 | tf_op jit(solution)/shard_map/ppermute | solution.py:255
where the time goes:
time: 42.2 us; the launch traced here: 42 us
  Pallas kernels  16 us (38%)
  starting transfers between devices  14.8 us (35%)
  waiting for transfers between devices  10.4 us (25%)
  local copies, waits for them, and re-layouts  0.66 us (2%)
    ppermute x13, starting transfers between devices, swap(): return lax.ppermute(array, axis, [(i, i ^ distance) for i in range(size)])  14.8 us
    ppermute x13, waiting for transfers between devices, swap(): return lax.ppermute(array, axis, [(i, i ^ distance) for i in range(size)])  10.4 us
    pallas_call x1, Pallas kernels, per_device(): pl.pallas_call(lambda *refs: context_kernel(False, *refs), out_shape=[wid...  5.63 us
    pallas_call x1, Pallas kernels, per_device(): pl.pallas_call(own_kernel, out_shape=[jax.ShapeDtypeStruct((count, featur...  5.33 us
    pallas_call x1, Pallas kernels, per_device(): pl.pallas_call(lambda *refs: pack_kernel(capacity, *refs), out_shape=[pie...  1.75 us
    pallas_call x1, Pallas kernels, per_device(): pl.pallas_call(lambda *refs: context_kernel(True, *refs), out_shape=[jax....  1.4 us
    pallas_call x1, Pallas kernels, per_device(): pl.pallas_call(value_kernel, out_shape=jax.ShapeDtypeStruct((count, featu...  1.36 us
  transfers between devices with their start and end apart: 13, of which 4 were waited for; matrix products, arithmetic and copies ran while one was open for 0% of the time, Pallas kernels for 29%

commit v1 on v0

--- a/solution.py
+++ b/solution.py
@@ -52,9 +52,8 @@
     ]
     for copy in copies:
         copy.start()
-    for copy in copies:
+    for copy in copies[:2]:
         copy.wait()
-    rows = rows_ref[...]
     row = iota((2 * half, slots), 0)
     level = (row % half) // ROW_BLK
     before = (iota((slots, slots), 0) < iota((slots, slots), 1)).astype(jnp.float32)
@@ -65,33 +64,44 @@
     base = (line // half) * tokens + line % ROW_BLK
     column = iota((2 * half, 2 * tokens), 1)
     member = iota(wanted_all.shape, 0)
-    for distance, out_ref in enumerate(out_refs):
-        group = me ^ distance
-        here = member == group
+    choices = []
+    for distance in range(len(out_refs)):
+        here = member == (me ^ distance)
         wanted = jnp.sum(jnp.where(here, wanted_all, 0), axis=0, keepdims=True)
         blocks = jnp.sum(jnp.where(here, block_ref[...], 0), axis=0, keepdims=True)
         source = jnp.sum(jnp.where(wanted == level, blocks, 0), axis=1, keepdims=True)
-        out_ref[...] = pick(column == base + source * ROW_BLK, rows)
-
-
-def compact_kernel(capacity, me_ref, shard_ref, after_ref, *refs):
-    piece_refs, (keys_ref, values_ref) = refs[:-2], refs[-2:]
-    me = me_ref[0]
-    slots = shard_ref.shape[1]
+        choices.append((column == base + source * ROW_BLK).astype(jnp.bfloat16))
+    choice = jnp.concatenate(choices, axis=0)
+    for copy in copies[2:]:
+        copy.wait()
+    picked = pick(choice, rows_ref[...])
+    for distance, out_ref in enumerate(out_refs):
+        out_ref[...] = picked[distance * 2 * half : (distance + 1) * 2 * half]
+
+
+def context_choice(capacity, me, shards_all, piece_rows):
+    slots = shards_all.shape[1]
     half = capacity * ROW_BLK
     tokens = slots * ROW_BLK
-    pieces = jnp.concatenate([piece_ref[...] for piece_ref in piece_refs], axis=0)
-    here = iota(shard_ref.shape, 0) == me
-    shards = jnp.sum(jnp.where(here, shard_ref[...], 0), axis=0, keepdims=True)
-    slot = iota((tokens, slots), 0) // ROW_BLK
-    lane = iota((tokens, slots), 1)
+    here = iota(shards_all.shape, 0) == me
+    shards = jnp.sum(jnp.where(here, shards_all, 0), axis=0, keepdims=True)
+    line = iota((2 * tokens, slots), 0)
+    slot = (line % tokens) // ROW_BLK
+    lane = iota((2 * tokens, slots), 1)
     named = jnp.sum(jnp.where(lane == slot, shards, 0), axis=1, keepdims=True)
     level = jnp.sum(((shards == named) & (lane < slot)).astype(jnp.int32), axis=1, keepdims=True)
-    inside = iota((tokens, 1), 0) % ROW_BLK
+    line = line[:, :1]
+    inside = line % ROW_BLK + (line // tokens) * half
     target = (named ^ me) * (2 * half) + level * ROW_BLK + inside
-    column = iota((tokens, pieces.shape[0]), 1)
-    keys_ref[...] = pick(column == target, pieces)
-    values_ref[...] = pick(column == target + half, pieces)
+    return (iota((2 * tokens, piece_rows), 1) == target).astype(jnp.bfloat16)
+
+
+def compact_kernel(choice_ref, *refs):
+    piece_refs, (keys_ref, values_ref) = refs[:-2], refs[-2:]
+    pieces = jnp.concatenate([piece_ref[...] for piece_ref in piece_refs], axis=0)
+    picked = pick(choice_ref[...], pieces)
+    keys_ref[...] = picked[: keys_ref.shape[0]]
+    values_ref[...] = picked[keys_ref.shape[0] :]
 
 
 def weigh(weights, values):
@@ -101,7 +111,10 @@
 
 
 def own_kernel(
+    capacity,
+    me_ref,
     lengths_ref,
+    shard_ref,
     q_hbm,
     keys_hbm,
     values_hbm,
@@ -110,6 +123,7 @@
     acc_ref,
     largest_ref,
     total_ref,
+    choice_ref,
     mask_ref,
     keys_ref,
     values_ref,
@@ -124,6 +138,7 @@
     ]
     for copy in copies:
         copy.start()
+    choice_ref[...] = context_choice(capacity, me_ref[0], shard_ref[...], choice_ref.shape[1])
     count, features = query_ref.shape
     blocks = count // BLK
     starts = [max(0, block - 1) * BLK for block in range(blocks)]
@@ -291,11 +306,14 @@
     pieces = [sent[0]]
     for distance in range(1, groups):
         pieces.append(swap(sent[distance], "dp", distance))
-    query, acc, largest, total = pl.pallas_call(
-        own_kernel,
-        out_shape=[jax.ShapeDtypeStruct((count, features), bf16)] + [wide] * 3,
-        in_specs=[SMEM] + [HBM] * 3 + [VMEM],
-        out_specs=[VMEM] * 4,
+    piece_rows = groups * piece.shape[0]
+    query, acc, largest, total, choice = pl.pallas_call(
+        lambda *refs: own_kernel(capacity, *refs),
+        out_shape=[jax.ShapeDtypeStruct((count, features), bf16)]
+        + [wide] * 3
+        + [jax.ShapeDtypeStruct((2 * tokens, piece_rows), bf16)],
+        in_specs=[SMEM] * 2 + [VMEM] + [HBM] * 3 + [VMEM],
+        out_specs=[VMEM] * 5,
         scratch_shapes=[
             pltpu.VMEM((count, 2 * BLK), jnp.float32),
             pltpu.VMEM((count, features), bf16),
@@ -310,16 +328,16 @@
             transcendentals=2 * count * BLK * heads,
             bytes_accessed=20 * count * features,
         ),
-    )(variant_blocks[0, 0], hbm(queries[0]), hbm(own_keys[0]), hbm(own_values[0]), sent[0])
+    )(me, variant_blocks[0, 0], ret_shard, hbm(queries[0]), hbm(own_keys[0]), hbm(own_values[0]), sent[0])
     row_block = jax.ShapeDtypeStruct((tokens, features), bf16)
     keys, values = pl.pallas_call(
-        lambda *refs: compact_kernel(capacity, *refs),
+        compact_kernel,
         out_shape=[row_block] * 2,
-        in_specs=[SMEM] + [VMEM] * (2 + groups),
+        in_specs=[VMEM] * (1 + groups),
         out_specs=[VMEM] * 2,
         name="compact",
         compiler_params=PARAMS,
-    )(me, ret_shard, total, *pieces)
+    )(choice, *pieces)
     far = []
     distance = columns // 2
     while distance > 1:

time: 42.2 us -> 41.6 us (0.986)
  waiting for transfers between devices: 10.4 us -> 9.66 us
  Pallas kernels: 16 us -> 15.3 us
  local copies, waits for them, and re-layouts: 0.66 us -> 1.34 us
    ppermute x13, waiting for transfers between devices: 10.4 us -> 9.66 us  [swap(): return lax.ppermute(array, axis, [(i, i ^ distance) for i in range(size)])]
    unnamed x4, local copies, waits for them, and re-layouts: 0.66 us -> 1.34 us
  transfers between devices with their start and end apart: 13 -> 13, of which waited for: 4 -> 4; matrix products, arithmetic and copies ran while one was open for 0% -> 0% of each run, Pallas kernels for 29% -> 30%
where the time goes in v1:
time: 41.6 us; the launch traced here: 41.4 us
  Pallas kernels  15.3 us (37%)
  starting transfers between devices  14.8 us (36%)
  waiting for transfers between devices  9.66 us (23%)
  local copies, waits for them, and re-layouts  1.34 us (3%)
    ppermute x13, starting transfers between devices, swap(): return lax.ppermute(array, axis, [(i, i ^ distance) for i in range(size)])  14.8 us
    ppermute x13, waiting for transfers between devices, swap(): return lax.ppermute(array, axis, [(i, i ^ distance) for i in range(size)])  9.66 us
    pallas_call x1, Pallas kernels, per_device(): pl.pallas_call(lambda *refs: context_kernel(False, *refs), out_shape=[wid...  5.57 us
    pallas_call x1, Pallas kernels, per_device(): pl.pallas_call(lambda *refs: own_kernel(capacity, *refs), out_shape=[jax....  5.39 us
    pallas_call x1, Pallas kernels, per_device(): pl.pallas_call(lambda *refs: context_kernel(True, *refs), out_shape=[jax....  1.39 us
    pallas_call x1, Pallas kernels, per_device(): pl.pallas_call(lambda *refs: pack_kernel(capacity, *refs), out_shape=[pie...  1.38 us
    pallas_call x1, Pallas kernels, per_device(): pl.pallas_call(value_kernel, out_shape=jax.ShapeDtypeStruct((count, featu...  1.35 us
    unnamed x4, local copies, waits for them, and re-layouts  1.34 us
  transfers between devices with their start and end apart: 13, of which 4 were waited for; matrix products, arithmetic and copies ran while one was open for 0% of the time, Pallas kernels for 30%

profile of v1, /device:TPU:17, one launch (start us, length us, event | category | flops | bytes accessed | tf_op | source)
XLA Modules:
  0.0 41.4 jit_solution(4730049441355298842)
XLA Ops:
  0.0 1.4 %pack.1 = (bf16[32,1280]{1,0:T(8,128)(2,1)S(1)}, bf16[32,1280]{1,0:T(8,128)(2,1)S(1)}, bf16[32,1280]{1,0:T(8,128)(2,1)S(1)}, bf16[32,1280]{1,0:T(8,128)(2,1)S(1)...) custom-call(s32[1]{0:T(128)} %bitcast.refs_0_, ...), custom_call_target="tpu_custom_call" | custom-call | tf_op jit(solution)/shard_map/pack/pallas_call | solution.py:292
  1.4 1.3 %collective-permute-start = (bf16[32,1280]{1,0:T(8,128)(2,1)S(1)}, bf16[32,1280]{1,0:T(8,128)(2,1)S(1)}, u32[]{:S(2)}, u32[]{:S(2)}) collective-permute-start(bf16[32,1280]{1,0:T(8,128)(2,1)S(1)} %get-tuple-element.32), channel_id=1, source_target_pairs={{0,4},{4,0},{8,12},{12,8},{16,20},{20,16},{24,28},{28,24},{1,5},{5... | collective-permute-start | bytes 245768 | tf_op jit(solution)/shard_map/ppermute | solution.py:270
  2.7 1.3 %collective-permute-start.1 = (bf16[32,1280]{1,0:T(8,128)(2,1)S(1)}, bf16[32,1280]{1,0:T(8,128)(2,1)S(1)}, u32[]{:S(2)}, u32[]{:S(2)}) collective-permute-start(bf16[32,1280]{1,0:T(8,128)(2,1)S(1)} %get-tuple-element.33), channel_id=1, source_target_pairs={{0,8},{4,12},{8,0},{12,4},{16,24},{20,28},{24,16},{28,20},{1,9},{5... | collective-permute-start | bytes 245768 | tf_op jit(solution)/shard_map/ppermute | solution.py:270
  4.0 0.1 collective-permute-start.2
  4.1 3.3 %collective-permute-start.4 = (bf16[32,1280]{1,0:T(8,128)(2,1)S(1)}, bf16[32,1280]{1,0:T(8,128)(2,1)S(1)}, u32[]{:S(2)}, u32[]{:S(2)}) collective-permute-start(bf16[32,1280]{1,0:T(8,128)(2,1)S(1)} %get-tuple-element.36), channel_id=1, source_target_pairs={{0,20},{4,16},{8,28},{12,24},{16,4},{20,0},{24,12},{28,8},{1,21},{... | collective-permute-start | bytes 245768 | tf_op jit(solution)/shard_map/ppermute | solution.py:270
  7.4 0.0 collective-permute-done.refs_1_
  7.4 0.2 collective-permute-start.5
  7.6 1.3 %collective-permute-start.6 = (bf16[32,1280]{1,0:T(8,128)(2,1)S(1)}, bf16[32,1280]{1,0:T(8,128)(2,1)S(1)}, u32[]{:S(2)}, u32[]{:S(2)}) collective-permute-start(bf16[32,1280]{1,0:T(8,128)(2,1)S(1)} %get-tuple-element.38), channel_id=1, source_target_pairs={{0,28},{4,24},{8,20},{12,16},{16,12},{20,8},{24,4},{28,0},{1,29},{... | collective-permute-start | bytes 245768 | tf_op jit(solution)/shard_map/ppermute | solution.py:270
  8.8 0.7 %copy-done = s32[8,16]{1,0:T(8,128)S(1)} copy-done((s32[8,16]{1,0:T(8,128)S(1)}, s32[8,16]{1,0:T(8,128)}, u32[]{:S(2)}) %copy-start) | copy-done | bytes 536
  9.5 0.7 %copy-done.1 = s32[1,1,6]{2,1,0:T(1,128)S(1)} copy-done((s32[1,1,6]{2,1,0:T(1,128)S(1)}, s32[1,1,6]{2,1,0:T(1,128)}, u32[]{:S(2)}) %copy-start.1) | copy-done | bytes 48
  10.2 5.4 %own.1 = (bf16[512,1280]{1,0:T(8,128)(2,1)S(1)}, f32[512,1280]{1,0:T(8,128)S(1)}, f32[512,1280]{1,0:T(8,128)S(1)}, f32[512,1280]{1,0:T(8,128)S(1)}, bf16[128,256]{1,0:T(8,128)(2,1)S(1)}) custom-call(s32[1]{0:T(128)} %bitcast.refs_0_, s32[6]{0:T(128)S(1)} %bitcast.8, s32[8,16]{1,0:T(8,128)S(1)} %copy-done, bf16[512,1280]{1,0:T(8,128)(2,1)} %bitcast.9, ...), custom_call_target="tpu_custom_call" | custom-call | flops 335544320 | bytes 13107200 | tf_op jit(solution)/shard_map/own/pallas_call | solution.py:310
  15.6 3.2 %collective-permute-done.5.refs_6_ = bf16[32,1280]{1,0:T(8,128)(2,1)S(1)} collective-permute-done((bf16[32,1280]{1,0:T(8,128)(2,1)S(1)}, bf16[32,1280]{1,0:T(8,128)(2,1)S(1)}, u32[]{:S(2)}, u32[]{:S(2)}) %collective-permute-start.5) | collective-permute-done | bytes 81952 | tf_op jit(solution)/shard_map/ppermute | solution.py:270
  18.8 3.6 %collective-permute-done.6.refs_7_ = bf16[32,1280]{1,0:T(8,128)(2,1)S(1)} collective-permute-done((bf16[32,1280]{1,0:T(8,128)(2,1)S(1)}, bf16[32,1280]{1,0:T(8,128)(2,1)S(1)}, u32[]{:S(2)}, u32[]{:S(2)}) %collective-permute-start.6) | collective-permute-done | bytes 81952 | tf_op jit(solution)/shard_map/ppermute | solution.py:270
  22.4 0.3 compact.1
  22.6 1.3 %collective-permute-start.9 = (bf16[64,1280]{1,0:T(8,128)(2,1)S(1)}, bf16[64,1280]{1,0:T(8,128)(2,1)S(1)}, u32[]{:S(2)}, u32[]{:S(2)}) collective-permute-start(bf16[64,1280]{1,0:T(8,128)(2,1)S(1)} %get-tuple-element.39.refs_4_), channel_id=1, source_target_pairs={{0,2},{1,3},{2,0},{3,1},{4,6},{5,7},{6,4},{7,5},{8,10},{9,11},{10,... | collective-permute-start | bytes 491528 | tf_op jit(solution)/shard_map/ppermute | solution.py:270
  23.9 0.2 collective-permute-start.11
  24.2 1.3 %collective-permute-start.7 = (bf16[64,1280]{1,0:T(8,128)(2,1)S(1)}, bf16[64,1280]{1,0:T(8,128)(2,1)S(1)}, u32[]{:S(2)}, u32[]{:S(2)}) collective-permute-start(bf16[64,1280]{1,0:T(8,128)(2,1)S(1)} %get-tuple-element.39.refs_4_), channel_id=1, source_target_pairs={{0,1},{1,0},{2,3},{3,2},{4,5},{5,4},{6,7},{7,6},{8,9},{9,8},{10,11... | collective-permute-start | bytes 491528 | tf_op jit(solution)/shard_map/ppermute | solution.py:270
  25.5 2.2 %collective-permute-done.9.refs_4_ = bf16[64,1280]{1,0:T(8,128)(2,1)S(1)} collective-permute-done((bf16[64,1280]{1,0:T(8,128)(2,1)S(1)}, bf16[64,1280]{1,0:T(8,128)(2,1)S(1)}, u32[]{:S(2)}, u32[]{:S(2)}) %collective-permute-start.9) | collective-permute-done | bytes 163872 | tf_op jit(solution)/shard_map/ppermute | solution.py:270
  27.7 2.8 %collective-permute-start.10 = (bf16[64,1280]{1,0:T(8,128)(2,1)S(1)}, bf16[64,1280]{1,0:T(8,128)(2,1)S(1)}, u32[]{:S(2)}, u32[]{:S(2)}) collective-permute-start(bf16[64,1280]{1,0:T(8,128)(2,1)S(1)} %collective-permute-done.9.refs_4_), channel_id=1, source_target_pairs={{0,1},{1,0},{2,3},{3,2},{4,5},{5,4},{6,7},{7,6},{8,9},{9,8},{10,11... | collective-permute-start | bytes 491528 | tf_op jit(solution)/shard_map/ppermute | solution.py:270
  30.5 0.7 %collective-permute-done.11.refs_0_ = bf16[64,1280]{1,0:T(8,128)(2,1)S(1)} collective-permute-done((bf16[64,1280]{1,0:T(8,128)(2,1)S(1)}, bf16[64,1280]{1,0:T(8,128)(2,1)S(1)}, u32[]{:S(2)}, u32[]{:S(2)}) %collective-permute-start.11) | collective-permute-done | bytes 163872 | tf_op jit(solution)/shard_map/ppermute | solution.py:270
  31.2 1.6 %collective-permute-start.12 = (bf16[64,1280]{1,0:T(8,128)(2,1)S(1)}, bf16[64,1280]{1,0:T(8,128)(2,1)S(1)}, u32[]{:S(2)}, u32[]{:S(2)}) collective-permute-start(bf16[64,1280]{1,0:T(8,128)(2,1)S(1)} %collective-permute-done.11.refs_0_), channel_id=1, source_target_pairs={{0,1},{1,0},{2,3},{3,2},{4,5},{5,4},{6,7},{7,6},{8,9},{9,8},{10,11... | collective-permute-start | bytes 491528 | tf_op jit(solution)/shard_map/ppermute | solution.py:270
  32.8 5.6 %near.1 = (f32[512,1280]{1,0:T(8,128)S(1)}, f32[512,1280]{1,0:T(8,128)S(1)}, f32[512,1280]{1,0:T(8,128)S(1)}) custom-call(bf16[512,1280]{1,0:T(8,128)(2,1)S(1)} %get-tuple-element.27.refs_0_, f32[512,1280]{1,0:T(8,128)S(1)} %get-tuple-element.28.refs_1_, f32[512,1280]{1,0:T(8,128)S(1)} %get-tuple-element.29.refs_2_, ...), custom_call_target="tpu_custom_call", output_to_operand_aliasing={{1}: (2, {})} | custom-call | tf_op jit(solution)/shard_map/near/pallas_call | solution.py:350
  38.4 1.4 %score.1 = (bf16[10,512,128]{2,1,0:T(8,128)(2,1)S(1)}, f32[512,1280]{1,0:T(8,128)S(1)}, f32[512,1280]{1,0:T(8,128)S(1)}, f32[512,1280]{1,0:T(8,128)S(1)}) custom-call(bf16[512,1280]{1,0:T(8,128)(2,1)S(1)} %get-tuple-element.27.refs_0_, f32[512,1280]{1,0:T(8,128)S(1)} %get-tuple-element.41.refs_1_, ...), custom_call_target="tpu_custom_call", output_to_operand_aliasing={{1}: (1, {}), {2}: (2, {})} | custom-call | tf_op jit(solution)/shard_map/score/pallas_call | solution.py:359
  39.8 1.4 %value.1 = bf16[512,1280]{1,0:T(8,128)(2,1)} custom-call(f32[512,1280]{1,0:T(8,128)S(1)} %get-tuple-element.44.scaled_ref, bf16[10,512,128]{2,1,0:T(8,128)(2,1)S(1)} %get-tuple-element.45.weights_ref, f32[512,1280]{1,0:T(8,128)S(1)} %get-tuple-element.46.inverse_ref, bf16[64,1280]{1,0:T(8,128)(2,1)S(1)} %collective-permute-done.11.refs_0_, ...), custom_call_target="tpu_custom_call" | custom-call | tf_op jit(solution)/shard_map/value/pallas_call | solution.py:368
  (12 shorter events, 0.0 us)
Async XLA Ops:
  1.4 6.0 %collective-permute-start = (bf16[32,1280]{1,0:T(8,128)(2,1)S(1)}, bf16[32,1280]{1,0:T(8,128)(2,1)S(1)}, u32[]{:S(2)}, u32[]{:S(2)}) collective-permute-start(bf16[32,1280]{1,0:T(8,128)(2,1)S(1)} %get-tuple-element.32), channel_id=1, source_target_pairs={{0,4},{4,0},{8,12},{12,8},{16,20},{20,16},{24,28},{28,24},{1,5},{5... | collective-permute-start | bytes 245768 | tf_op jit(solution)/shard_map/ppermute | solution.py:270
  2.7 4.9 %collective-permute-start.1 = (bf16[32,1280]{1,0:T(8,128)(2,1)S(1)}, bf16[32,1280]{1,0:T(8,128)(2,1)S(1)}, u32[]{:S(2)}, u32[]{:S(2)}) collective-permute-start(bf16[32,1280]{1,0:T(8,128)(2,1)S(1)} %get-tuple-element.33), channel_id=1, source_target_pairs={{0,8},{4,12},{8,0},{12,4},{16,24},{20,28},{24,16},{28,20},{1,9},{5... | collective-permute-start | bytes 245768 | tf_op jit(solution)/shard_map/ppermute | solution.py:270
  4.0 11.6 %collective-permute-start.2 = (bf16[32,1280]{1,0:T(8,128)(2,1)S(1)}, bf16[32,1280]{1,0:T(8,128)(2,1)S(1)}, u32[]{:S(2)}, u32[]{:S(2)}) collective-permute-start(bf16[32,1280]{1,0:T(8,128)(2,1)S(1)} %get-tuple-element.34), channel_id=1, source_target_pairs={{0,12},{4,8},{8,4},{12,0},{16,28},{20,24},{24,20},{28,16},{1,13},{... | collective-permute-start | bytes 245768 | tf_op jit(solution)/shard_map/ppermute | solution.py:270
  4.1 11.5 %collective-permute-start.3 = (bf16[32,1280]{1,0:T(8,128)(2,1)S(1)}, bf16[32,1280]{1,0:T(8,128)(2,1)S(1)}, u32[]{:S(2)}, u32[]{:S(2)}) collective-permute-start(bf16[32,1280]{1,0:T(8,128)(2,1)S(1)} %get-tuple-element.35), channel_id=1, source_target_pairs={{0,16},{4,20},{8,24},{12,28},{16,0},{20,4},{24,8},{28,12},{1,17},{... | collective-permute-start | bytes 245768 | tf_op jit(solution)/shard_map/ppermute | solution.py:270
  4.1 11.5 %collective-permute-start.4 = (bf16[32,1280]{1,0:T(8,128)(2,1)S(1)}, bf16[32,1280]{1,0:T(8,128)(2,1)S(1)}, u32[]{:S(2)}, u32[]{:S(2)}) collective-permute-start(bf16[32,1280]{1,0:T(8,128)(2,1)S(1)} %get-tuple-element.36), channel_id=1, source_target_pairs={{0,20},{4,16},{8,28},{12,24},{16,4},{20,0},{24,12},{28,8},{1,21},{... | collective-permute-start | bytes 245768 | tf_op jit(solution)/shard_map/ppermute | solution.py:270
  7.4 11.4 %collective-permute-start.5 = (bf16[32,1280]{1,0:T(8,128)(2,1)S(1)}, bf16[32,1280]{1,0:T(8,128)(2,1)S(1)}, u32[]{:S(2)}, u32[]{:S(2)}) collective-permute-start(bf16[32,1280]{1,0:T(8,128)(2,1)S(1)} %get-tuple-element.37), channel_id=1, source_target_pairs={{0,24},{4,28},{8,16},{12,20},{16,8},{20,12},{24,0},{28,4},{1,25},{... | collective-permute-start | bytes 245768 | tf_op jit(solution)/shard_map/ppermute | solution.py:270
  7.6 14.8 %collective-permute-start.6 = (bf16[32,1280]{1,0:T(8,128)(2,1)S(1)}, bf16[32,1280]{1,0:T(8,128)(2,1)S(1)}, u32[]{:S(2)}, u32[]{:S(2)}) collective-permute-start(bf16[32,1280]{1,0:T(8,128)(2,1)S(1)} %get-tuple-element.38), channel_id=1, source_target_pairs={{0,28},{4,24},{8,20},{12,16},{16,12},{20,8},{24,4},{28,0},{1,29},{... | collective-permute-start | bytes 245768 | tf_op jit(solution)/shard_map/ppermute | solution.py:270
  8.8 0.7 %copy-start = (s32[8,16]{1,0:T(8,128)S(1)}, s32[8,16]{1,0:T(8,128)}, u32[]{:S(2)}) copy-start(s32[8,16]{1,0:T(8,128)} %refs_2_.3) | copy-start | bytes 1540
  9.5 0.7 %copy-start.1 = (s32[1,1,6]{2,1,0:T(1,128)S(1)}, s32[1,1,6]{2,1,0:T(1,128)}, u32[]{:S(2)}) copy-start(s32[1,1,6]{2,1,0:T(1,128)} %param.11) | copy-start | bytes 76
  22.6 5.1 %collective-permute-start.9 = (bf16[64,1280]{1,0:T(8,128)(2,1)S(1)}, bf16[64,1280]{1,0:T(8,128)(2,1)S(1)}, u32[]{:S(2)}, u32[]{:S(2)}) collective-permute-start(bf16[64,1280]{1,0:T(8,128)(2,1)S(1)} %get-tuple-element.39.refs_4_), channel_id=1, source_target_pairs={{0,2},{1,3},{2,0},{3,1},{4,6},{5,7},{6,4},{7,5},{8,10},{9,11},{10,... | collective-permute-start | bytes 491528 | tf_op jit(solution)/shard_map/ppermute | solution.py:270
  23.9 7.3 %collective-permute-start.11 = (bf16[64,1280]{1,0:T(8,128)(2,1)S(1)}, bf16[64,1280]{1,0:T(8,128)(2,1)S(1)}, u32[]{:S(2)}, u32[]{:S(2)}) collective-permute-start(bf16[64,1280]{1,0:T(8,128)(2,1)S(1)} %get-tuple-element.40.refs_6_), channel_id=1, source_target_pairs={{0,2},{1,3},{2,0},{3,1},{4,6},{5,7},{6,4},{7,5},{8,10},{9,11},{10,... | collective-permute-start | bytes 491528 | tf_op jit(solution)/shard_map/ppermute | solution.py:270
  24.2 8.7 %collective-permute-start.7 = (bf16[64,1280]{1,0:T(8,128)(2,1)S(1)}, bf16[64,1280]{1,0:T(8,128)(2,1)S(1)}, u32[]{:S(2)}, u32[]{:S(2)}) collective-permute-start(bf16[64,1280]{1,0:T(8,128)(2,1)S(1)} %get-tuple-element.39.refs_4_), channel_id=1, source_target_pairs={{0,1},{1,0},{2,3},{3,2},{4,5},{5,4},{6,7},{7,6},{8,9},{9,8},{10,11... | collective-permute-start | bytes 491528 | tf_op jit(solution)/shard_map/ppermute | solution.py:270
  25.5 7.3 %collective-permute-start.8 = (bf16[64,1280]{1,0:T(8,128)(2,1)S(1)}, bf16[64,1280]{1,0:T(8,128)(2,1)S(1)}, u32[]{:S(2)}, u32[]{:S(2)}) collective-permute-start(bf16[64,1280]{1,0:T(8,128)(2,1)S(1)} %get-tuple-element.40.refs_6_), channel_id=1, source_target_pairs={{0,1},{1,0},{2,3},{3,2},{4,5},{5,4},{6,7},{7,6},{8,9},{9,8},{10,11... | collective-permute-start | bytes 491528 | tf_op jit(solution)/shard_map/ppermute | solution.py:270
  27.7 10.7 %collective-permute-start.10 = (bf16[64,1280]{1,0:T(8,128)(2,1)S(1)}, bf16[64,1280]{1,0:T(8,128)(2,1)S(1)}, u32[]{:S(2)}, u32[]{:S(2)}) collective-permute-start(bf16[64,1280]{1,0:T(8,128)(2,1)S(1)} %collective-permute-done.9.refs_4_), channel_id=1, source_target_pairs={{0,1},{1,0},{2,3},{3,2},{4,5},{5,4},{6,7},{7,6},{8,9},{9,8},{10,11... | collective-permute-start | bytes 491528 | tf_op jit(solution)/shard_map/ppermute | solution.py:270
  31.2 8.6 %collective-permute-start.12 = (bf16[64,1280]{1,0:T(8,128)(2,1)S(1)}, bf16[64,1280]{1,0:T(8,128)(2,1)S(1)}, u32[]{:S(2)}, u32[]{:S(2)}) collective-permute-start(bf16[64,1280]{1,0:T(8,128)(2,1)S(1)} %collective-permute-done.11.refs_0_), channel_id=1, source_target_pairs={{0,1},{1,0},{2,3},{3,2},{4,5},{5,4},{6,7},{7,6},{8,9},{9,8},{10,11... | collective-permute-start | bytes 491528 | tf_op jit(solution)/shard_map/ppermute | solution.py:270
